TPU v7x, 256 devices: a whole 4x4x8 slice. The times are simulated.
256 devices in a mesh: dp: 2 (over core), expert: 4 (over x), tensor: 32 (over z, y).
Axes of the slice: x: 4, y: 4, z: 8, core: 2. Of those that a mesh axis runs over, the one named last changes fastest.
Arguments:
- tokens: bfloat16 [1024, 3072], P(('dp', 'expert')), may hold values from -6 to 6
- cotangent: bfloat16 [1024, 3072], P(('dp', 'expert')), may hold values from -6 to 6
- gate_weights: bfloat16 [1024, 2], P(('dp', 'expert')), may hold values from 0.099609375 to 0.8984375
- expert_ids: int32 [1024, 2], P(('dp', 'expert')), may hold values from 0 to 3, all different within a row; in each aligned block of 128 rows (0 to 127, 128 to 255, ...) at most 96 rows name the same one
- w_gate: bfloat16 [4, 3072, 8192], P('expert', 'dp', 'tensor'), may hold values from -0.109375 to 0.109375
- w_up: bfloat16 [4, 3072, 8192], P('expert', 'dp', 'tensor'), may hold values from -0.109375 to 0.109375
- w_down: bfloat16 [4, 3072, 8192], P('expert', 'dp', 'tensor'), may hold values from -0.0625 to 0.0625
Outputs:
- input_grad: bfloat16 [1024, 3072], P(('dp', 'expert'))
- gate_grad: bfloat16 [1024, 2], P(('dp', 'expert'))
- grad_gate: bfloat16 [4, 3072, 8192], P('expert', 'dp', 'tensor')
- grad_up: bfloat16 [4, 3072, 8192], P('expert', 'dp', 'tensor')
- grad_down: bfloat16 [4, 3072, 8192], P('expert', 'dp', 'tensor')
Inputs may be any that keep to these rules, and one draw needn't show every extreme that they name: `expert_ids`: each token names 2 different experts. Among the 128 tokens of one block, no expert is named more than 96 times, and in some blocks one expert is named exactly 96 times.
All inputs are finite; a program needn't handle non-finite values.
Results may differ from a plain program's by a relative error of at most 0.025.
Values may be sent and summed in bfloat16 or wider, within the bound.
No kernel may reach another device: no remote copies, remote signals or barrier semaphores. Data moves between devices by JAX's collectives and lax.ppermute only.
A program may use at most 64 MiB of HBM per device.

v0:
```python
import jax
import jax.numpy as jnp
from jax import lax
from jax.sharding import PartitionSpec as P


def slot_numbers(expert_ids, experts):
    labels = lax.broadcasted_iota(jnp.int32, (1, 1, experts), 2)
    onehot = (expert_ids[:, :, None] == labels).astype(jnp.int32).reshape(-1, experts)
    earlier = jnp.cumsum(onehot, axis=0) - onehot
    return jnp.sum(earlier * onehot, axis=1)


def entry_table(expert_ids, experts, capacity):
    flat_slot = slot_numbers(expert_ids, experts)
    target = expert_ids.reshape(-1) * capacity + flat_slot
    entry_count = expert_ids.shape[0] * expert_ids.shape[1]
    entries = jnp.full((experts * capacity,), entry_count, jnp.int32)
    entries = entries.at[target].set(jnp.arange(entry_count, dtype=jnp.int32))
    return (target, entries)


def fill_buffers(tokens, cotangent, gate_weights, entries):
    model_width = tokens.shape[1]
    zero_row = jnp.zeros((1, model_width), tokens.dtype)
    token_rows = entries // 2
    token_pad = jnp.concatenate([tokens, zero_row], 0)
    grad_pad = jnp.concatenate([cotangent, zero_row], 0)
    weight_pad = jnp.concatenate([gate_weights.reshape(-1), jnp.zeros((2,), gate_weights.dtype)], 0)
    return (token_pad[token_rows], grad_pad[token_rows], weight_pad[entries])


def on_device(tokens, cotangent, gate_weights, expert_ids, w_gate, w_up, w_down):
    experts = lax.axis_size("expert")
    tok_count = tokens.shape[0]
    model_width = tokens.shape[1]
    capacity = tok_count * 3 // experts
    target, entries = entry_table(expert_ids, experts, capacity)
    x_flat, dy_flat, g_flat = fill_buffers(tokens, cotangent, gate_weights, entries)
    x_buf = x_flat.reshape(experts, capacity, model_width)
    dy_buf = dy_flat.reshape(experts, capacity, model_width)
    g_buf = g_flat.reshape(experts, capacity)
    gathered = (
        lax.all_gather(w_gate, "dp", axis=1, tiled=True),
        lax.all_gather(w_up, "dp", axis=1, tiled=True),
        lax.all_gather(w_down, "dp", axis=1, tiled=True),
    )
    gate_full = gathered[0][0]
    up_full = gathered[1][0]
    down_full = gathered[2][0]
    x_in, dy_in, g_in = (
        lax.all_to_all(x_buf, "expert", split_axis=0, concat_axis=0, tiled=True),
        lax.all_to_all(dy_buf, "expert", split_axis=0, concat_axis=0, tiled=True),
        lax.all_to_all(g_buf, "expert", split_axis=0, concat_axis=0, tiled=True),
    )
    rows_x = x_in.reshape(-1, model_width)
    rows_dy = dy_in.reshape(-1, model_width)
    factor = g_in.reshape(-1).astype(jnp.float32)[:, None]
    inner = (((1,), (1,)), ((), ()))
    outer = (((0,), (0,)), ((), ()))
    gate_pre = jnp.dot(rows_x, gate_full, preferred_element_type=jnp.float32)
    up_pre = jnp.dot(rows_x, up_full, preferred_element_type=jnp.float32)
    sigma = jax.nn.sigmoid(gate_pre)
    active = gate_pre * sigma
    hidden = (active * up_pre).astype(jnp.bfloat16)
    back = jnp.dot(rows_dy, down_full, preferred_element_type=jnp.float32)
    slot_gate = jnp.sum(hidden.astype(jnp.float32) * back, axis=1)
    hidden_grad = factor * back
    d_pre_gate = (hidden_grad * up_pre * sigma * (1.0 + gate_pre * (1.0 - sigma))).astype(
        jnp.bfloat16
    )
    d_pre_up = (hidden_grad * active).astype(jnp.bfloat16)
    scaled = (factor * rows_dy.astype(jnp.float32)).astype(jnp.bfloat16)
    slot_input = lax.dot_general(
        d_pre_gate, gate_full, inner, preferred_element_type=jnp.float32
    ) + lax.dot_general(d_pre_up, up_full, inner, preferred_element_type=jnp.float32)
    part_gate = lax.dot_general(rows_x, d_pre_gate, outer, preferred_element_type=jnp.float32)
    part_up = lax.dot_general(rows_x, d_pre_up, outer, preferred_element_type=jnp.float32)
    part_down = lax.dot_general(scaled, hidden, outer, preferred_element_type=jnp.float32)
    slot_input = slot_input.reshape(experts, capacity, model_width)
    slot_gate = slot_gate.reshape(experts, capacity)
    summed = (
        lax.psum_scatter(
            slot_input.astype(jnp.bfloat16), "tensor", scatter_dimension=1, tiled=True
        ).astype(jnp.float32),
        lax.psum_scatter(
            slot_gate.astype(jnp.bfloat16), "tensor", scatter_dimension=1, tiled=True
        ).astype(jnp.float32),
    )
    input_share = summed[0].astype(jnp.bfloat16)
    gate_share = summed[1].astype(jnp.bfloat16)
    joined = (
        lax.all_gather(input_share, "tensor", axis=1, tiled=True),
        lax.all_gather(gate_share, "tensor", axis=1, tiled=True),
    )
    returned = (
        lax.all_to_all(joined[0], "expert", split_axis=0, concat_axis=0, tiled=True),
        lax.all_to_all(joined[1], "expert", split_axis=0, concat_axis=0, tiled=True),
    )
    picked = returned[0].reshape(-1, model_width)[target].reshape(tok_count, 2, model_width)
    input_grad = jnp.sum(picked.astype(jnp.float32), axis=1).astype(jnp.bfloat16)
    gate_grad = returned[1].reshape(-1)[target].reshape(tok_count, 2)
    totals = (
        lax.psum_scatter(
            part_gate[None].astype(jnp.bfloat16), "dp", scatter_dimension=1, tiled=True
        ).astype(jnp.float32),
        lax.psum_scatter(
            part_up[None].astype(jnp.bfloat16), "dp", scatter_dimension=1, tiled=True
        ).astype(jnp.float32),
        lax.psum_scatter(
            part_down[None].astype(jnp.bfloat16), "dp", scatter_dimension=1, tiled=True
        ).astype(jnp.float32),
    )
    return (
        input_grad,
        gate_grad,
        totals[0].astype(jnp.bfloat16),
        totals[1].astype(jnp.bfloat16),
        totals[2].astype(jnp.bfloat16),
    )


def solution(mesh):
    return jax.shard_map(
        on_device,
        mesh=mesh,
        in_specs=(
            P(("dp", "expert"), None),
            P(("dp", "expert"), None),
            P(("dp", "expert"), None),
            P(("dp", "expert"), None),
            P("expert", "dp", "tensor"),
            P("expert", "dp", "tensor"),
            P("expert", "dp", "tensor"),
        ),
        out_specs=(
            P(("dp", "expert"), None),
            P(("dp", "expert"), None),
            P("expert", "dp", "tensor"),
            P("expert", "dp", "tensor"),
            P("expert", "dp", "tensor"),
        ),
        check_vma=False,
    )
```

profile of v0, /device:TPU:8, one launch (start us, length us, event | category | flops | bytes accessed | tf_op | source)
XLA Modules:
  0.0 429.8 jit_solution(11514104356832466018)
XLA Ops:
  10.9 1.2 reduce-window.6
  12.5 1.4 scatter_custom_fusion
  14.0 2.8 gather_fusion
  17.4 4.3 all-to-all-start
  21.8 3.6 gather_fusion.2
  25.4 1.5 all-to-all-done
  26.9 3.6 all-to-all-start.2
  32.6 3.6 gather_fusion.1
  36.1 22.7 %all-to-all-done.2 = bf16[4,96,3072]{2,1,0:T(8,128)(2,1)S(1)} async-done(((bf16[4,96,3072]{2,1,0:T(8,128)(2,1)}), bf16[4,96,3072]{2,1,0:T(8,128)(2,1)S(1)}, u32[]{:S(2)}, u32[]{:S(2)}) %all-to-all-start.2) | async-done | bytes 2359328 | tf_op jit(solution)/shard_map/all_to_all | solution.py:52
  58.8 4.5 %all-to-all-start.1 = ((bf16[4,96,3072]{2,1,0:T(8,128)(2,1)}), bf16[4,96,3072]{2,1,0:T(8,128)(2,1)}, u32[]{:S(2)}, u32[]{:S(2)}) async-start(bf16[4,96,3072]{2,1,0:T(8,128)(2,1)} %bitcast.73), calls=%async_computation.1 | async-start | bytes 4718592 | tf_op jit(solution)/shard_map/all_to_all | solution.py:53
  64.2 2.4 fusion.6
  66.7 2.4 fusion.9
  69.1 15.3 %all-gather.6.cloned.1.call-done = bf16[1,3072,256]{2,1,0:T(8,128)(2,1)} async-done(((bf16[1,1536,256]{2,1,0:T(8,128)(2,1)}), bf16[1,3072,256]{2,1,0:T(8,128)(2,1)}) %all-gather.6.cloned.1.call-update) | async-done | bytes 1572880 | tf_op jit(solution)/shard_map/all_gather | solution.py:46
  84.4 6.3 %all-to-all-done.1 = bf16[4,96,3072]{2,1,0:T(8,128)(2,1)} async-done(((bf16[4,96,3072]{2,1,0:T(8,128)(2,1)}), bf16[4,96,3072]{2,1,0:T(8,128)(2,1)}, u32[]{:S(2)}, u32[]{:S(2)}) %all-to-all-start.1) | async-done | bytes 2359328 | tf_op jit(solution)/shard_map/all_to_all | solution.py:53
  90.7 4.1 multiply_reduce_fusion
  97.0 3.3 copy.43
  102.2 153.1 %all-reduce.7.cloned.1.call-done = bf16[4,96,3072]{2,0,1:T(4,128)(2,1)} async-done(((bf16[4,96,3072]{2,0,1:T(4,128)(2,1)}), bf16[4,96,3072]{2,0,1:T(4,128)(2,1)}) %all-reduce.7.cloned.1.call-update) | async-done | bytes 2359312
  255.4 1.5 constant_dynamic-slice_fusion
  257.0 4.0 fusion.2
  261.0 2.2 fusion.1
  263.3 2.2 fusion
  265.6 71.4 %all-reduce.4 = bf16[4,96]{1,0:T(4,128)(2,1)S(1)} all-reduce(bf16[4,96]{1,0:T(4,128)(2,1)S(1)} %convert_element_type.89), channel_id=3, replica_groups=mesh['dp'=2,'expert'=4,'tensor'=32] {'tensor'}, use_global_device_ids=true, to_apply=%region_7.8.clone | all-reduce | flops 384 | bytes 1536
  337.2 42.6 %all-gather = bf16[32,3,4]{2,1,0:T(4,128)(2,1)S(1)} all-gather(bf16[1,3,4]{2,1,0:T(4,128)(2,1)S(1)} %bitcast.80), channel_id=1, replica_groups=mesh['dp'=2,'expert'=4,'tensor'=32] {'tensor'}, dimensions={0}, use_global_device_ids=true | all-gather | bytes 792 | tf_op jit(solution)/shard_map/all_gather | solution.py:94
  380.5 4.3 all-to-all-start.4
  384.8 3.9 copy.44
  388.7 1.4 all-to-all-done.4
  390.1 3.6 all-to-all-start.3
  393.8 1.9 gather_fusion.4
  396.6 15.0 %all-to-all-done.3 = bf16[4,96,3072]{2,1,0:T(8,128)(2,1)S(1)} async-done(((bf16[4,96,3072]{2,1,0:T(8,128)(2,1)}), bf16[4,96,3072]{2,1,0:T(8,128)(2,1)S(1)}, u32[]{:S(2)}, u32[]{:S(2)}) %all-to-all-start.3) | async-done | bytes 2359328 | tf_op jit(solution)/shard_map/all_to_all | solution.py:97
  411.6 2.7 gather_fusion.3
  414.3 3.5 reshape.114
  417.8 5.1 %reduce_sum.34 = bf16[128,3072]{1,0:T(8,128)(2,1)} reduce(bf16[128,2,3072]{2,1,0:T(2,128)(2,1)S(1)} %reshape.114, bf16[]{:T(256)} %constant.12.clone.1), dimensions={1}, to_apply=%region_5.6 | reduce | flops 393216 | bytes 2359298 | tf_op jit(solution)/shard_map/reduce_sum | solution.py:101
  (72 shorter events, 13.2 us)
Async XLA Ops:
  7.2 14.6 %copy-start.2 = (bf16[128,3072]{1,0:T(8,128)(2,1)S(1)}, bf16[128,3072]{1,0:T(8,128)(2,1)}, u32[]{:S(2)}) copy-start(bf16[128,3072]{1,0:T(8,128)(2,1)} %param.7) | copy-start | bytes 2359300
  7.2 57.0 %all-gather.10.cloned.1.call-start = ((), (), s32[]{:S(2)}) async-start(), calls=%async_computation.10 | async-start | bytes 2359296 | tf_op jit(solution)/shard_map/all_gather | solution.py:44
  17.4 9.5 %all-to-all-start = ((bf16[4,1,96]{2,1,0:T(2,128)(2,1)}), bf16[4,1,96]{2,1,0:T(2,128)(2,1)S(1)}, u32[]{:S(2)}, u32[]{:S(2)}) async-start(bf16[4,1,96]{2,1,0:T(2,128)(2,1)} %all_to_all.28), calls=%async_computation | async-start | bytes 4096 | tf_op jit(solution)/shard_map/all_to_all | solution.py:54
  26.9 31.8 %all-to-all-start.2 = ((bf16[4,96,3072]{2,1,0:T(8,128)(2,1)}), bf16[4,96,3072]{2,1,0:T(8,128)(2,1)S(1)}, u32[]{:S(2)}, u32[]{:S(2)}) async-start(bf16[4,96,3072]{2,1,0:T(8,128)(2,1)} %bitcast.74), calls=%async_computation.2 | async-start | bytes 4718592 | tf_op jit(solution)/shard_map/all_to_all | solution.py:52
  30.6 36.1 %all-gather.8.cloned.1.call-start = ((), (), s32[]{:S(2)}) async-start(), calls=%async_computation.9 | async-start | bytes 2359296 | tf_op jit(solution)/shard_map/all_gather | solution.py:45
  58.8 32.0 %all-to-all-start.1 = ((bf16[4,96,3072]{2,1,0:T(8,128)(2,1)}), bf16[4,96,3072]{2,1,0:T(8,128)(2,1)}, u32[]{:S(2)}, u32[]{:S(2)}) async-start(bf16[4,96,3072]{2,1,0:T(8,128)(2,1)} %bitcast.73), calls=%async_computation.1 | async-start | bytes 4718592 | tf_op jit(solution)/shard_map/all_to_all | solution.py:53
  63.3 21.1 %all-gather.6.cloned.1.call-start = ((), (), s32[]{:S(2)}) async-start(), calls=%async_computation.8 | async-start | bytes 2359296 | tf_op jit(solution)/shard_map/all_gather | solution.py:46
  64.0 191.3 %all-reduce.7.cloned.1.call-start = ((), (), s32[]{:S(2)}) async-start(), calls=%async_computation.15 | async-start | bytes 4718592
  90.7 4.1 copy-start
  94.8 1.4 copy-start.1
  100.3 0.7 copy-start.3
  100.3 156.7 %copy-start.4 = (bf16[384,256]{0,1:T(8,128)(2,1)S(1)}, bf16[384,256]{0,1:T(8,128)(2,1)}, u32[]{:S(2)}) copy-start(bf16[384,256]{0,1:T(8,128)(2,1)} %get-tuple-element.21) | copy-start | bytes 589828
  100.3 284.5 %all-gather.12.cloned.1.call-start = ((), (), s32[]{:S(2)}) async-start(), calls=%async_computation.11 | async-start | bytes 2433024 | tf_op jit(solution)/shard_map/all_gather | solution.py:93
  256.9 166.0 %reduce-scatter.9.cloned.1.call-start = ((), (), s32[]{:S(2)}) async-start(), calls=%async_computation.14 | async-start | bytes 2359296 | tf_op jit(solution)/shard_map/reduce_scatter | solution.py:110
  261.0 162.0 %reduce-scatter.7.cloned.1.call-start = ((), (), s32[]{:S(2)}) async-start(), calls=%async_computation.13 | async-start | bytes 2359296 | tf_op jit(solution)/shard_map/reduce_scatter | solution.py:107
  263.3 159.6 %reduce-scatter.5.cloned.1.call-start = ((), (), s32[]{:S(2)}) async-start(), calls=%async_computation.12 | async-start | bytes 2359296 | tf_op jit(solution)/shard_map/reduce_scatter | solution.py:104
  380.5 9.6 %all-to-all-start.4 = ((bf16[4,1,96]{2,1,0:T(2,128)(2,1)}), bf16[4,1,96]{2,1,0:T(2,128)(2,1)S(1)}, u32[]{:S(2)}, u32[]{:S(2)}) async-start(bf16[4,1,96]{2,1,0:T(2,128)(2,1)} %copy.47), calls=%async_computation.4 | async-start | bytes 4096 | tf_op jit(solution)/shard_map/all_to_all | solution.py:98
  390.1 21.5 %all-to-all-start.3 = ((bf16[4,96,3072]{2,1,0:T(8,128)(2,1)}), bf16[4,96,3072]{2,1,0:T(8,128)(2,1)S(1)}, u32[]{:S(2)}, u32[]{:S(2)}) async-start(bf16[4,96,3072]{2,1,0:T(8,128)(2,1)} %copy.44), calls=%async_computation.3 | async-start | bytes 4718592 | tf_op jit(solution)/shard_map/all_to_all | solution.py:97
Sparse Core Ops, SparseCore 0:
  9.8 18.0 all-gather.9
  33.2 18.4 all-gather.7
  65.9 18.4 all-gather.5
  100.5 154.8 all-reduce.6
  258.4 75.8 all-gather.11
  337.2 13.1 reduce-scatter.8
  353.4 15.7 reduce-scatter.6
  372.3 15.7 reduce-scatter.4
where the time goes:
time: 431 us; the launch traced here: 430 us
  waiting for transfers between devices  218 us (51%)
  blocking collectives  114 us (26%)
  local copies, waits for them, and re-layouts  36.2 us (8%)
  starting transfers between devices  20.8 us (5%)
  matrix products  19 us (4%)
  between operations  15 us (3%)
  other arithmetic  7.21 us (2%)
    unnamed x9, waiting for transfers between devices  155 us
    unnamed x1, blocking collectives  71.4 us
    all_gather x1, blocking collectives, on_device(): lax.all_gather(gate_share, 'tensor', axis=1, tiled=True)  42.6 us
    all_to_all x1, waiting for transfers between devices, on_device(): lax.all_to_all(x_buf, 'expert', split_axis=0, concat_axis=0, tiled=True)  22.7 us
    all_gather x1, waiting for transfers between devices, on_device(): lax.all_gather(w_down, 'dp', axis=1, tiled=True)  15.3 us
    all_to_all x1, waiting for transfers between devices, on_device(): lax.all_to_all(joined[0], 'expert', split_axis=0, concat_axis=0, tiled=True)  15 us
    gather x3, local copies, waits for them, and re-layouts, fill_buffers(): return (token_pad[token_rows], grad_pad[token_rows], weight_pad[entries])  9.97 us
  transfers between devices with their start and end apart: 13, of which 7 were waited for; matrix products, arithmetic and copies ran while one was open for 12% of the time, Pallas kernels for 0%

commit v1 on v0

--- a/solution.py
+++ b/solution.py
@@ -91,7 +91,10 @@
     gate_share = summed[1].astype(jnp.bfloat16)
     joined = (
         lax.all_gather(input_share, "tensor", axis=1, tiled=True),
-        lax.all_gather(gate_share, "tensor", axis=1, tiled=True),
+        jnp.concatenate(
+            lax.all_to_all(jnp.stack([gate_share] * lax.axis_size("tensor")), "tensor", 0, 0),
+            axis=1,
+        ),
     )
     returned = (
         lax.all_to_all(joined[0], "expert", split_axis=0, concat_axis=0, tiled=True),

time: 431 us -> 404 us (0.937)
  blocking collectives: 114 us -> 87.4 us
    all_gather x1 -> x0, blocking collectives: 42.6 us -> none  [on_device(): lax.all_gather(gate_share, 'tensor', axis=1, tiled=True)]
    all_to_all x0 -> x1, blocking collectives: none -> 16 us  [on_device(): lax.all_to_all(jnp.stack([gate_share] * lax.axis_size('tensor')), 'tensor...]
where the time goes in v1:
time: 404 us; the launch traced here: 403 us
  waiting for transfers between devices  218 us (54%)
  blocking collectives  87.4 us (22%)
  local copies, waits for them, and re-layouts  36 us (9%)
  starting transfers between devices  21 us (5%)
  matrix products  19 us (5%)
  between operations  15 us (4%)
  other arithmetic  7.21 us (2%)
    unnamed x9, waiting for transfers between devices  155 us
    unnamed x1, blocking collectives  71.4 us
    all_to_all x1, waiting for transfers between devices, on_device(): lax.all_to_all(x_buf, 'expert', split_axis=0, concat_axis=0, tiled=True)  22.7 us
    all_to_all x1, blocking collectives, on_device(): lax.all_to_all(jnp.stack([gate_share] * lax.axis_size('tensor')), 'tensor...  16 us
    all_gather x1, waiting for transfers between devices, on_device(): lax.all_gather(w_down, 'dp', axis=1, tiled=True)  15.3 us
    all_to_all x1, waiting for transfers between devices, on_device(): lax.all_to_all(joined[0], 'expert', split_axis=0, concat_axis=0, tiled=True)  15 us
    gather x3, local copies, waits for them, and re-layouts, fill_buffers(): return (token_pad[token_rows], grad_pad[token_rows], weight_pad[entries])  9.97 us
  transfers between devices with their start and end apart: 13, of which 7 were waited for; matrix products, arithmetic and copies ran while one was open for 12% of the time, Pallas kernels for 0%

profile of v1, /device:TPU:8, one launch (start us, length us, event | category | flops | bytes accessed | tf_op | source)
XLA Modules:
  0.0 403.2 jit_solution(6042005174773656829)
XLA Ops:
  10.9 1.2 reduce-window.6
  12.5 1.4 scatter_custom_fusion
  14.0 2.8 gather_fusion
  17.4 4.3 %all-to-all-start = ((bf16[4,1,96]{2,1,0:T(2,128)(2,1)}), bf16[4,1,96]{2,1,0:T(2,128)(2,1)S(1)}, u32[]{:S(2)}, u32[]{:S(2)}) async-start(bf16[4,1,96]{2,1,0:T(2,128)(2,1)} %all_to_all.32), calls=%async_computation | async-start | bytes 4096 | tf_op jit(solution)/shard_map/all_to_all | solution.py:54
  21.8 3.6 gather_fusion.2
  25.4 1.5 all-to-all-done
  26.9 3.6 all-to-all-start.2
  32.6 3.6 gather_fusion.1
  36.1 22.7 %all-to-all-done.2 = bf16[4,96,3072]{2,1,0:T(8,128)(2,1)S(1)} async-done(((bf16[4,96,3072]{2,1,0:T(8,128)(2,1)}), bf16[4,96,3072]{2,1,0:T(8,128)(2,1)S(1)}, u32[]{:S(2)}, u32[]{:S(2)}) %all-to-all-start.2) | async-done | bytes 2359328 | tf_op jit(solution)/shard_map/all_to_all | solution.py:52
  58.8 4.5 %all-to-all-start.1 = ((bf16[4,96,3072]{2,1,0:T(8,128)(2,1)}), bf16[4,96,3072]{2,1,0:T(8,128)(2,1)}, u32[]{:S(2)}, u32[]{:S(2)}) async-start(bf16[4,96,3072]{2,1,0:T(8,128)(2,1)} %bitcast.68), calls=%async_computation.1 | async-start | bytes 4718592 | tf_op jit(solution)/shard_map/all_to_all | solution.py:53
  64.2 2.4 fusion.6
  66.7 2.4 fusion.9
  69.1 15.3 %all-gather.5.cloned.1.call-done = bf16[1,3072,256]{2,1,0:T(8,128)(2,1)} async-done(((bf16[1,1536,256]{2,1,0:T(8,128)(2,1)}), bf16[1,3072,256]{2,1,0:T(8,128)(2,1)}) %all-gather.5.cloned.1.call-update) | async-done | bytes 1572880 | tf_op jit(solution)/shard_map/all_gather | solution.py:46
  84.4 6.3 %all-to-all-done.1 = bf16[4,96,3072]{2,1,0:T(8,128)(2,1)} async-done(((bf16[4,96,3072]{2,1,0:T(8,128)(2,1)}), bf16[4,96,3072]{2,1,0:T(8,128)(2,1)}, u32[]{:S(2)}, u32[]{:S(2)}) %all-to-all-start.1) | async-done | bytes 2359328 | tf_op jit(solution)/shard_map/all_to_all | solution.py:53
  90.7 4.1 %multiply_reduce_fusion = (bf16[384]{0:T(512)(128)(2,1)S(1)}, bf16[384,256]{0,1:T(8,128)(2,1)}, bf16[384,256]{0,1:T(8,128)(2,1)S(1)}, bf16[384,256]{0,1:T(8,128)(2,1)S(1)}) fusion(f32[384,256]{0,1:T(8,128)S(1)} %fusion.9, f32[384,256]{0,1:T(8,128)S(1)} %fusion.6, f32[384]{0:T(512)S(1)} %reshape.125, bf16[384,3072]{1,0:T(8,128)(2,1)} %bitcast.5, ...), kind=kOutput, calls=%fused_computation.24 | convolution fusion | flops 605847168 | bytes 5310720 | tf_op jit(solution)/shard_map/dot_general | solution.py:66
  97.0 3.3 copy.40
  102.2 153.1 %all-reduce.7.cloned.1.call-done = bf16[4,96,3072]{2,0,1:T(4,128)(2,1)} async-done(((bf16[4,96,3072]{2,0,1:T(4,128)(2,1)}), bf16[4,96,3072]{2,0,1:T(4,128)(2,1)}) %all-reduce.7.cloned.1.call-update) | async-done | bytes 2359312
  255.4 1.5 constant_dynamic-slice_fusion.1
  257.0 4.0 fusion.2
  261.0 2.2 fusion.1
  263.3 2.2 fusion
  265.6 71.4 %all-reduce.4 = bf16[4,96]{1,0:T(4,128)(2,1)S(1)} all-reduce(bf16[4,96]{1,0:T(4,128)(2,1)S(1)} %convert_element_type.89), channel_id=3, replica_groups=mesh['dp'=2,'expert'=4,'tensor'=32] {'tensor'}, use_global_device_ids=true, to_apply=%region_7.8.clone | all-reduce | flops 384 | bytes 1536
  337.1 16.0 %all_to_all.40 = bf16[32,4,3]{2,1,0:T(4,128)(2,1)S(1)} all-to-all(bf16[32,4,3]{2,1,0:T(4,128)(2,1)S(1)} %stack.2), channel_id=1, replica_groups=mesh['dp'=2,'expert'=4,'tensor'=32] {'tensor'}, dimensions={0} | all-to-all | bytes 1536 | tf_op jit(solution)/shard_map/all_to_all | solution.py:95
  353.8 4.2 %all-to-all-start.5 = ((bf16[4,1,96]{2,1,0:T(2,128)(2,1)}), bf16[4,1,96]{2,1,0:T(2,128)(2,1)S(1)}, u32[]{:S(2)}, u32[]{:S(2)}) async-start(bf16[4,1,96]{2,1,0:T(2,128)(2,1)} %all_to_all.33), calls=%async_computation.5 | async-start | bytes 4096 | tf_op jit(solution)/shard_map/all_to_all | solution.py:101
  358.1 3.8 copy.41
  361.9 1.5 all-to-all-done.5
  363.4 3.8 all-to-all-start.3
  367.3 1.9 gather_fusion.4
  370.0 15.0 %all-to-all-done.3 = bf16[4,96,3072]{2,1,0:T(8,128)(2,1)S(1)} async-done(((bf16[4,96,3072]{2,1,0:T(8,128)(2,1)}), bf16[4,96,3072]{2,1,0:T(8,128)(2,1)S(1)}, u32[]{:S(2)}, u32[]{:S(2)}) %all-to-all-start.3) | async-done | bytes 2359328 | tf_op jit(solution)/shard_map/all_to_all | solution.py:100
  385.1 2.7 gather_fusion.3
  387.8 3.5 reshape.121
  391.3 5.1 %reduce_sum.34 = bf16[128,3072]{1,0:T(8,128)(2,1)} reduce(bf16[128,2,3072]{2,1,0:T(2,128)(2,1)S(1)} %reshape.121, bf16[]{:T(256)} %constant.12.clone.1), dimensions={1}, to_apply=%region_5.6 | reduce | flops 393216 | bytes 2359298 | tf_op jit(solution)/shard_map/reduce_sum | solution.py:104
  (71 shorter events, 13.1 us)
Async XLA Ops:
  7.2 14.6 %copy-start.2 = (bf16[128,3072]{1,0:T(8,128)(2,1)S(1)}, bf16[128,3072]{1,0:T(8,128)(2,1)}, u32[]{:S(2)}) copy-start(bf16[128,3072]{1,0:T(8,128)(2,1)} %param.7) | copy-start | bytes 2359300
  7.2 57.0 %all-gather.9.cloned.1.call-start = ((), (), s32[]{:S(2)}) async-start(), calls=%async_computation.11 | async-start | bytes 2359296 | tf_op jit(solution)/shard_map/all_gather | solution.py:44
  17.4 9.5 %all-to-all-start = ((bf16[4,1,96]{2,1,0:T(2,128)(2,1)}), bf16[4,1,96]{2,1,0:T(2,128)(2,1)S(1)}, u32[]{:S(2)}, u32[]{:S(2)}) async-start(bf16[4,1,96]{2,1,0:T(2,128)(2,1)} %all_to_all.32), calls=%async_computation | async-start | bytes 4096 | tf_op jit(solution)/shard_map/all_to_all | solution.py:54
  26.9 31.8 %all-to-all-start.2 = ((bf16[4,96,3072]{2,1,0:T(8,128)(2,1)}), bf16[4,96,3072]{2,1,0:T(8,128)(2,1)S(1)}, u32[]{:S(2)}, u32[]{:S(2)}) async-start(bf16[4,96,3072]{2,1,0:T(8,128)(2,1)} %bitcast.69), calls=%async_computation.2 | async-start | bytes 4718592 | tf_op jit(solution)/shard_map/all_to_all | solution.py:52
  30.6 36.1 %all-gather.7.cloned.1.call-start = ((), (), s32[]{:S(2)}) async-start(), calls=%async_computation.10 | async-start | bytes 2359296 | tf_op jit(solution)/shard_map/all_gather | solution.py:45
  58.8 32.0 %all-to-all-start.1 = ((bf16[4,96,3072]{2,1,0:T(8,128)(2,1)}), bf16[4,96,3072]{2,1,0:T(8,128)(2,1)}, u32[]{:S(2)}, u32[]{:S(2)}) async-start(bf16[4,96,3072]{2,1,0:T(8,128)(2,1)} %bitcast.68), calls=%async_computation.1 | async-start | bytes 4718592 | tf_op jit(solution)/shard_map/all_to_all | solution.py:53
  63.3 21.1 %all-gather.5.cloned.1.call-start = ((), (), s32[]{:S(2)}) async-start(), calls=%async_computation.9 | async-start | bytes 2359296 | tf_op jit(solution)/shard_map/all_gather | solution.py:46
  64.0 191.3 %all-reduce.7.cloned.1.call-start = ((), (), s32[]{:S(2)}) async-start(), calls=%async_computation.16 | async-start | bytes 4718592
  90.7 4.1 %copy-start = (bf16[1,3072,256]{2,1,0:T(8,128)(2,1)S(1)}, bf16[1,3072,256]{2,1,0:T(8,128)(2,1)}, u32[]{:S(2)}) copy-start(bf16[1,3072,256]{2,1,0:T(8,128)(2,1)} %all-gather.9.cloned.1.call-done) | copy-start | bytes 4718596
  94.8 1.4 copy-start.1
  100.3 0.7 copy-start.3
  100.3 156.7 %copy-start.4 = (bf16[384,256]{0,1:T(8,128)(2,1)S(1)}, bf16[384,256]{0,1:T(8,128)(2,1)}, u32[]{:S(2)}) copy-start(bf16[384,256]{0,1:T(8,128)(2,1)} %get-tuple-element.21) | copy-start | bytes 589828
  100.3 257.8 %all-gather.11.cloned.1.call-start = ((), (), s32[]{:S(2)}) async-start(), calls=%async_computation.12 | async-start | bytes 2433024 | tf_op jit(solution)/shard_map/all_gather | solution.py:93
  256.9 139.5 %reduce-scatter.9.cloned.1.call-start = ((), (), s32[]{:S(2)}) async-start(), calls=%async_computation.15 | async-start | bytes 2359296 | tf_op jit(solution)/shard_map/reduce_scatter | solution.py:113
  261.0 135.4 %reduce-scatter.7.cloned.1.call-start = ((), (), s32[]{:S(2)}) async-start(), calls=%async_computation.14 | async-start | bytes 2359296 | tf_op jit(solution)/shard_map/reduce_scatter | solution.py:110
  263.3 133.1 %reduce-scatter.5.cloned.1.call-start = ((), (), s32[]{:S(2)}) async-start(), calls=%async_computation.13 | async-start | bytes 2359296 | tf_op jit(solution)/shard_map/reduce_scatter | solution.py:107
  353.8 9.5 %all-to-all-start.5 = ((bf16[4,1,96]{2,1,0:T(2,128)(2,1)}), bf16[4,1,96]{2,1,0:T(2,128)(2,1)S(1)}, u32[]{:S(2)}, u32[]{:S(2)}) async-start(bf16[4,1,96]{2,1,0:T(2,128)(2,1)} %all_to_all.33), calls=%async_computation.5 | async-start | bytes 4096 | tf_op jit(solution)/shard_map/all_to_all | solution.py:101
  363.4 21.7 %all-to-all-start.3 = ((bf16[4,96,3072]{2,1,0:T(8,128)(2,1)}), bf16[4,96,3072]{2,1,0:T(8,128)(2,1)S(1)}, u32[]{:S(2)}, u32[]{:S(2)}) async-start(bf16[4,96,3072]{2,1,0:T(8,128)(2,1)} %copy.41), calls=%async_computation.3 | async-start | bytes 4718592 | tf_op jit(solution)/shard_map/all_to_all | solution.py:100
Sparse Core Ops, SparseCore 0:
  9.8 18.0 all-gather.8
  33.2 18.4 all-gather.6
  65.9 18.4 all-gather.4
  100.5 154.8 all-reduce.6
  258.4 75.9 all-gather.10
  337.3 13.0 reduce-scatter.8
  353.4 15.7 reduce-scatter.6
  372.3 15.7 reduce-scatter.4
